TPU v7x, 32 devices: a whole 2x2x4 slice. The times are simulated.
32 devices in a mesh: dp: 4 (over x, core), context: 2 (over y), tensor: 4 (over z).
Axes of the slice: x: 2, y: 2, z: 4, core: 2. Of those that a mesh axis runs over, the one named last changes fastest.
Arguments:
- layer_input: bfloat16 [4, 4096, 2048], P('dp', 'context'), may hold values from -6 to 6
- cotangent: bfloat16 [4, 4096, 2048], P('dp', 'context'), may hold values from -6 to 6
- w_qkv: bfloat16 [2048, 1536], P(('dp', 'context'), 'tensor'), may hold values from -0.125 to 0.125
- w_out: bfloat16 [1024, 2048], P('tensor', ('dp', 'context')), may hold values from -1.5 to 1.5
- attn_gain: bfloat16 [2048], P(('dp', 'context')), may hold values from 0.5 to 1.5
- qk_gain: float32 [2, 64], replicated, may hold values from 0.1 to 1.9
- w_gate: bfloat16 [2048, 5120], P(('dp', 'context'), 'tensor'), may hold values from -0.125 to 0.125
- w_up: bfloat16 [2048, 5120], P(('dp', 'context'), 'tensor'), may hold values from -0.125 to 0.125
- w_down: bfloat16 [5120, 2048], P('tensor', ('dp', 'context')), may hold values from -0.078125 to 0.078125
- ffn_gain: bfloat16 [2048], P(('dp', 'context')), may hold values from 0.5 to 1.5
- seg_ids: int32 [4, 4096], P('dp'), may hold values from 0 to 8, as said below
- pos_ids: int32 [4, 4096], P('dp'), may hold values from 0 to 2431, as said below
Outputs:
- layer_output: bfloat16 [4, 4096, 2048], P('dp', 'context')
- grad_input: bfloat16 [4, 4096, 2048], P('dp', 'context')
- grad_qkv: float32 [2048, 1536], P(('dp', 'context'), 'tensor')
- grad_out_proj: float32 [1024, 2048], P('tensor', ('dp', 'context'))
- grad_attn_gain: float32 [2048], P(('dp', 'context'))
- grad_qk_gain: float32 [2, 64], replicated
- grad_gate: float32 [2048, 5120], P(('dp', 'context'), 'tensor')
- grad_up: float32 [2048, 5120], P(('dp', 'context'), 'tensor')
- grad_down: float32 [5120, 2048], P('tensor', ('dp', 'context'))
- grad_ffn_gain: float32 [2048], P(('dp', 'context'))
Inputs may be any that keep to these rules, and one draw needn't show every extreme that they name: `seg_ids`: within each group the first 2048 tokens have id 0; the rest form 8 runs of consecutive tokens with ids 1 to 8 rising along the tokens, each run 1 to 384 tokens long, one of exactly 384 in every group. `pos_ids`: prompt token t has position t; the tokens of a continuation have positions 2048, 2049, ... in order.
All inputs are finite; a program needn't handle non-finite values.
Results may differ from a plain program's by a relative error of at most 0.024.
Values may be sent and summed in bfloat16 or wider, within the bound.
A program may use at most 256 MiB of HBM per device.

v0:
```python
import math
import jax
import jax.numpy as jnp
from jax import lax
from jax.sharding import PartitionSpec as P

HEADS = 16
KV_HEADS = 4
HEAD_DIM = 64
epsilon = 1e-06
rope_base = 10000.0


def norm_rows(values, gains):
    return values * lax.rsqrt(jnp.mean(values * values, axis=-1, keepdims=True) + epsilon) * gains


def rope_tables(positions, head_width):
    half_width = head_width // 2
    inverse = jnp.exp(
        -math.log(rope_base) * jnp.arange(half_width, dtype=jnp.float32) * 2.0 / head_width
    )
    angles = positions.astype(jnp.float32)[..., None] * inverse
    cosine_tab = jnp.concatenate([jnp.cos(angles), jnp.cos(angles)], axis=-1)
    sine_table = jnp.concatenate([jnp.sin(angles), jnp.sin(angles)], axis=-1)
    return (cosine_tab, sine_table)


def rotate(values, cosine_tab, sine_table):
    half_width = values.shape[-1] // 2
    lower_half = values[..., :half_width]
    upper_half = values[..., half_width:]
    return values * cosine_tab + jnp.concatenate([-upper_half, lower_half], axis=-1) * sine_table


def visible(query_pos, query_seg, key_pos, key_seg):
    same_run = (key_seg[None, :] == 0) | (key_seg[None, :] == query_seg[:, None])
    return (key_pos[None, :] <= query_pos[:, None]) & same_run


def mixed_silu(gate_in, up_in):
    return jax.nn.silu(gate_in) * up_in


def tensor_total(partial_term):
    return lax.psum(partial_term.astype(jnp.bfloat16), "tensor").astype(jnp.float32)


def body(
    layer_input,
    cotangent,
    w_qkv,
    w_out,
    attn_gain,
    qk_gain,
    w_gate,
    w_up,
    w_down,
    ffn_gain,
    seg_ids,
    pos_ids,
):
    group_count, local_len, model_width = layer_input.shape
    group_len = seg_ids.shape[1]
    kv_local = KV_HEADS // lax.axis_size("tensor")
    head_ratio = HEADS // KV_HEADS
    row_count = group_count * local_len
    score_scale = HEAD_DIM ** (-0.5)
    block_rows = min(local_len, 128)
    block_count = local_len // block_rows
    first_row = lax.axis_index("context") * local_len
    my_seg = lax.dynamic_slice_in_dim(seg_ids, first_row, local_len, 1)
    my_pos = lax.dynamic_slice_in_dim(pos_ids, first_row, local_len, 1)
    qkv_all, out_all, attn_gain_all = (
        lax.all_gather(w_qkv, ("dp", "context"), axis=0, tiled=True),
        lax.all_gather(w_out, ("dp", "context"), axis=1, tiled=True),
        lax.all_gather(attn_gain, ("dp", "context"), axis=0, tiled=True),
    )
    inputs = layer_input.astype(jnp.float32).reshape(row_count, model_width)
    normed = norm_rows(inputs, attn_gain_all.astype(jnp.float32))
    normed_low = normed.astype(jnp.bfloat16)
    joint = jnp.dot(normed_low, qkv_all, preferred_element_type=jnp.float32)
    joint = joint.reshape(group_count, local_len, kv_local, head_ratio + 2, HEAD_DIM)
    cosine_tab, sine_table = rope_tables(my_pos, HEAD_DIM)

    def prepare(query_raw, key_raw, gains_qk):
        query_rot = rotate(
            norm_rows(query_raw, gains_qk[0]),
            cosine_tab[:, :, None, None, :],
            sine_table[:, :, None, None, :],
        )
        key_rot = rotate(
            norm_rows(key_raw, gains_qk[1]), cosine_tab[:, :, None, :], sine_table[:, :, None, :]
        )
        return (query_rot, key_rot)

    query_raw = joint[:, :, :, :head_ratio]
    key_raw = joint[:, :, :, head_ratio]
    query_rot, key_rot = prepare(query_raw, key_raw, qk_gain)
    queries = query_rot.astype(jnp.bfloat16)
    kv_mine = jnp.stack([key_rot, joint[:, :, :, head_ratio + 1]], axis=3).astype(jnp.bfloat16)
    kv_mine = kv_mine.reshape(group_count, local_len, kv_local * 2 * HEAD_DIM)
    kv_group = lax.all_gather(kv_mine, "context", axis=1, tiled=True).reshape(
        group_count, group_len, kv_local, 2, HEAD_DIM
    )

    def block_scores(query_block, keys, allowed):
        scores = jnp.einsum("qkrd,tkd->qkrt", query_block, keys, preferred_element_type=jnp.float32)
        return jnp.where(allowed[:, None, None, :], scores * score_scale, -1e30)

    member = 0
    keys = kv_group[member, :, :, 0]
    values = kv_group[member, :, :, 1]
    key_pos = pos_ids[member]
    key_seg = seg_ids[member]

    def forward_block(block_items):
        query_block, query_pos, query_seg = block_items
        scores = block_scores(query_block, keys, visible(query_pos, query_seg, key_pos, key_seg))
        row_max = jnp.max(scores, axis=-1, keepdims=True)
        exp_scores = jnp.exp(scores - row_max)
        totals = jnp.sum(exp_scores, axis=-1, keepdims=True)
        probs = (exp_scores / totals).astype(jnp.bfloat16)
        result = jnp.einsum("qkrt,tkd->qkrd", probs, values, preferred_element_type=jnp.float32)
        return (result, row_max[..., 0] + jnp.log(totals[..., 0]))

    result, log_total = lax.map(
        forward_block,
        (
            queries[member].reshape(block_count, block_rows, kv_local, head_ratio, HEAD_DIM),
            my_pos[member].reshape(block_count, block_rows),
            my_seg[member].reshape(block_count, block_rows),
        ),
    )
    attended_list = [result]
    log_total_list = [log_total]
    attended_low = (
        jnp.stack(attended_list)
        .astype(jnp.bfloat16)
        .reshape(row_count, kv_local * head_ratio * HEAD_DIM)
    )
    attn_part = jnp.dot(attended_low, out_all, preferred_element_type=jnp.float32)
    gate_all, up_all, down_all, ffn_gain_all = (
        lax.all_gather(w_gate, ("dp", "context"), axis=0, tiled=True),
        lax.all_gather(w_up, ("dp", "context"), axis=0, tiled=True),
        lax.all_gather(w_down, ("dp", "context"), axis=1, tiled=True),
        lax.all_gather(ffn_gain, ("dp", "context"), axis=0, tiled=True),
    )
    resid = inputs + tensor_total(attn_part)
    normed_ffn_low = norm_rows(resid, ffn_gain_all.astype(jnp.float32)).astype(jnp.bfloat16)
    gate = jnp.dot(normed_ffn_low, gate_all, preferred_element_type=jnp.float32)
    up = jnp.dot(normed_ffn_low, up_all, preferred_element_type=jnp.float32)
    act_low = mixed_silu(gate, up).astype(jnp.bfloat16)
    ffn_part = jnp.dot(act_low, down_all, preferred_element_type=jnp.float32)
    result_out = (resid + tensor_total(ffn_part)).astype(jnp.bfloat16)
    gate_all, up_all, down_all, ffn_gain_all = (
        lax.all_gather(w_gate, ("dp", "context"), axis=0, tiled=True),
        lax.all_gather(w_up, ("dp", "context"), axis=0, tiled=True),
        lax.all_gather(w_down, ("dp", "context"), axis=1, tiled=True),
        lax.all_gather(ffn_gain, ("dp", "context"), axis=0, tiled=True),
    )
    qkv_all, out_all, attn_gain_all = (
        lax.all_gather(w_qkv, ("dp", "context"), axis=0, tiled=True),
        lax.all_gather(w_out, ("dp", "context"), axis=1, tiled=True),
        lax.all_gather(attn_gain, ("dp", "context"), axis=0, tiled=True),
    )
    cot_low = cotangent.reshape(row_count, model_width)
    grad_down = jnp.dot(act_low.T, cot_low, preferred_element_type=jnp.float32)
    act_grad = jnp.dot(cot_low, down_all.T, preferred_element_type=jnp.float32)
    _, silu_pull = jax.vjp(mixed_silu, gate, up)
    gate_grad, up_grad = silu_pull(act_grad)
    gate_grad = gate_grad.astype(jnp.bfloat16)
    up_grad = up_grad.astype(jnp.bfloat16)
    grad_gate = jnp.dot(normed_ffn_low.T, gate_grad, preferred_element_type=jnp.float32)
    grad_up = jnp.dot(normed_ffn_low.T, up_grad, preferred_element_type=jnp.float32)
    ffn_in_part = jnp.dot(gate_grad, gate_all.T, preferred_element_type=jnp.float32) + jnp.dot(
        up_grad, up_all.T, preferred_element_type=jnp.float32
    )
    ffn_in_grad = tensor_total(ffn_in_part)
    _, norm_ffn_pull = jax.vjp(norm_rows, resid, ffn_gain_all.astype(jnp.float32))
    resid_norm_grad, grad_ffn_gain = norm_ffn_pull(ffn_in_grad)
    resid_grad = cot_low.astype(jnp.float32) + resid_norm_grad
    branch_grad = resid_grad.astype(jnp.bfloat16)
    grad_out_proj = jnp.dot(attended_low.T, branch_grad, preferred_element_type=jnp.float32)
    attended_grad = jnp.dot(branch_grad, out_all.T, preferred_element_type=jnp.float32).astype(
        jnp.bfloat16
    )
    attended_grad = attended_grad.reshape(group_count, local_len, kv_local, head_ratio, HEAD_DIM)
    member = 0
    keys = kv_group[member, :, :, 0]
    values = kv_group[member, :, :, 1]
    key_pos = pos_ids[member]
    key_seg = seg_ids[member]

    def backward_block(carried, block_items):
        query_block, query_pos, query_seg, log_total, grad_block = block_items
        scores = block_scores(query_block, keys, visible(query_pos, query_seg, key_pos, key_seg))
        probs = jnp.exp(scores - log_total[..., None])
        prob_grad = jnp.einsum(
            "qkrd,tkd->qkrt", grad_block, values, preferred_element_type=jnp.float32
        )
        inner = jnp.sum(probs * prob_grad, axis=-1, keepdims=True)
        score_grad = (probs * (prob_grad - inner) * score_scale).astype(jnp.bfloat16)
        query_grad = jnp.einsum(
            "qkrt,tkd->qkrd", score_grad, keys, preferred_element_type=jnp.float32
        )
        key_total = carried[0] + jnp.einsum(
            "qkrt,qkrd->tkd", score_grad, query_block, preferred_element_type=jnp.float32
        )
        value_total = carried[1] + jnp.einsum(
            "qkrt,qkrd->tkd",
            probs.astype(jnp.bfloat16),
            grad_block,
            preferred_element_type=jnp.float32,
        )
        return ((key_total, value_total), query_grad)

    empty = jnp.zeros((group_len, kv_local, HEAD_DIM), jnp.float32)
    (key_total, value_total), query_grad = lax.scan(
        backward_block,
        (empty, empty),
        (
            queries[member].reshape(block_count, block_rows, kv_local, head_ratio, HEAD_DIM),
            my_pos[member].reshape(block_count, block_rows),
            my_seg[member].reshape(block_count, block_rows),
            log_total_list[member],
            attended_grad[member].reshape(block_count, block_rows, kv_local, head_ratio, HEAD_DIM),
        ),
    )
    query_grads = [query_grad.reshape(local_len, kv_local, head_ratio, HEAD_DIM)]
    key_grads = [key_total]
    value_grads = [value_total]
    kv_grad_group = jnp.stack([jnp.stack(key_grads), jnp.stack(value_grads)], axis=3)
    kv_grad_group = kv_grad_group.reshape(group_count, group_len, kv_local * 2 * HEAD_DIM)
    kv_grad = lax.psum_scatter(
        kv_grad_group.astype(jnp.bfloat16), "context", scatter_dimension=1, tiled=True
    ).astype(jnp.float32)
    kv_grad = kv_grad.reshape(group_count, local_len, kv_local, 2, HEAD_DIM)
    _, prepare_pull = jax.vjp(prepare, query_raw, key_raw, qk_gain)
    query_raw_grad, key_raw_grad, qk_gain_part = prepare_pull(
        (jnp.stack(query_grads), kv_grad[:, :, :, 0])
    )
    joint_grad = jnp.concatenate(
        [query_raw_grad, key_raw_grad[:, :, :, None], kv_grad[:, :, :, 1][:, :, :, None]], axis=3
    )
    joint_grad = joint_grad.astype(jnp.bfloat16).reshape(
        row_count, kv_local * (head_ratio + 2) * HEAD_DIM
    )
    grad_qkv = jnp.dot(normed_low.T, joint_grad, preferred_element_type=jnp.float32)
    in_part = jnp.dot(joint_grad, qkv_all.T, preferred_element_type=jnp.float32)
    in_grad = tensor_total(in_part)
    _, norm_in_pull = jax.vjp(norm_rows, inputs, attn_gain_all.astype(jnp.float32))
    input_norm_grad, grad_attn_gain = norm_in_pull(in_grad)
    grad_input = (resid_grad + input_norm_grad).astype(jnp.bfloat16)
    grad_input = grad_input.reshape(group_count, local_len, model_width)
    grad_qk_gain = lax.psum(qk_gain_part, ("dp", "context", "tensor"))
    grads = (grad_qkv, grad_out_proj, grad_attn_gain, grad_gate, grad_up, grad_down, grad_ffn_gain)
    shard_qkv, shard_out, shard_attn_gain, shard_gate, shard_up, shard_down, shard_ffn_gain = (
        lax.psum_scatter(
            grads[0].astype(jnp.bfloat16), ("dp", "context"), scatter_dimension=0, tiled=True
        ).astype(jnp.float32),
        lax.psum_scatter(
            grads[1].astype(jnp.bfloat16), ("dp", "context"), scatter_dimension=1, tiled=True
        ).astype(jnp.float32),
        lax.psum_scatter(
            grads[2].astype(jnp.bfloat16), ("dp", "context"), scatter_dimension=0, tiled=True
        ).astype(jnp.float32),
        lax.psum_scatter(
            grads[3].astype(jnp.bfloat16), ("dp", "context"), scatter_dimension=0, tiled=True
        ).astype(jnp.float32),
        lax.psum_scatter(
            grads[4].astype(jnp.bfloat16), ("dp", "context"), scatter_dimension=0, tiled=True
        ).astype(jnp.float32),
        lax.psum_scatter(
            grads[5].astype(jnp.bfloat16), ("dp", "context"), scatter_dimension=1, tiled=True
        ).astype(jnp.float32),
        lax.psum_scatter(
            grads[6].astype(jnp.bfloat16), ("dp", "context"), scatter_dimension=0, tiled=True
        ).astype(jnp.float32),
    )
    return (
        result_out.reshape(group_count, local_len, model_width),
        grad_input,
        shard_qkv,
        shard_out,
        shard_attn_gain,
        grad_qk_gain,
        shard_gate,
        shard_up,
        shard_down,
        shard_ffn_gain,
    )


def solution(mesh):
    return jax.shard_map(
        body,
        mesh=mesh,
        in_specs=(
            P("dp", "context", None),
            P("dp", "context", None),
            P(("dp", "context"), "tensor"),
            P("tensor", ("dp", "context")),
            P(("dp", "context")),
            P(),
            P(("dp", "context"), "tensor"),
            P(("dp", "context"), "tensor"),
            P("tensor", ("dp", "context")),
            P(("dp", "context")),
            P("dp", None),
            P("dp", None),
        ),
        out_specs=(
            P("dp", "context", None),
            P("dp", "context", None),
            P(("dp", "context"), "tensor"),
            P("tensor", ("dp", "context")),
            P(("dp", "context")),
            P(),
            P(("dp", "context"), "tensor"),
            P(("dp", "context"), "tensor"),
            P("tensor", ("dp", "context")),
            P(("dp", "context")),
        ),
        check_vma=False,
    )
```

profile of v0, /device:TPU:0, one launch (start us, length us, event | category | flops | bytes accessed | tf_op | source)
XLA Modules:
  0.0 2420.3 jit_solution(337184587082190026)
XLA Ops:
  8.6 14.2 all-gather
  31.0 7.3 all-gather.9.cloned.1.call-done
  40.9 6.5 fusion.85
  54.2 16.8 all-gather.11.cloned.1.call-done
  72.2 110.1 %while.27 = (s32[]{:T(128)}, bf16[16,128,1,4,64]{1,4,3,2,0:T(8,128)(2,1)}, f32[16,128,1,4]{1,3,2,0:T(4,128)}, s32[1,4096]{1,0:T(1,128)S(1)}, s32[16,128]{1,0:T(8...) while((s32[]{:T(128)}, ...), condition=%wide.region_6.7_spmd, body=%wide.region_3.6_spmd.sunk | while | flops 555748864 | bytes 27536516 | solution.py:127
  185.7 7.4 convolution_convert_fusion.2
  195.1 13.0 all-gather.1
  208.1 276.0 %all-reduce.14.cloned.1.call-done = bf16[2048,2048]{1,0:T(8,128)(2,1)} async-done(((bf16[2048,2048]{1,0:T(8,128)(2,1)}), bf16[2048,2048]{1,0:T(8,128)(2,1)}) %all-reduce.14.cloned.1.call-update) | async-done | bytes 8388624 | tf_op jit(solution)/shard_map/psum | solution.py:46
  484.1 8.5 multiply_reduce_fusion
  492.6 11.6 multiply_convert_fusion
  504.2 21.8 all-gather.17.cloned.1.call-done
  526.0 16.5 fusion.132
  542.5 26.4 %all-gather.15.cloned.1.call-done = bf16[2048,1280]{1,0:T(8,128)(2,1)} async-done(((bf16[256,1280]{1,0:T(8,128)(2,1)}), bf16[2048,1280]{1,0:T(8,128)(2,1)}) %all-gather.15.cloned.1.call-update) | async-done | bytes 5242896 | tf_op jit(solution)/shard_map/all_gather | solution.py:144
  568.9 16.6 fusion.131
  585.5 27.3 %all-gather.19.cloned.1.call-done = bf16[1280,2048]{1,0:T(8,128)(2,1)} async-done(((bf16[1280,256]{1,0:T(8,128)(2,1)}), bf16[1280,2048]{1,0:T(8,128)(2,1)}) %all-gather.19.cloned.1.call-update) | async-done | bytes 5242896 | tf_op jit(solution)/shard_map/all_gather | solution.py:146
  612.8 23.4 multiply_convert_fusion.1
  636.2 18.0 fusion.133
  654.2 19.0 add_convert_fusion
  673.4 290.9 %all-reduce.16.cloned.1.call-done = bf16[2048,2048]{1,0:T(8,128)(2,1)} async-done(((bf16[2048,2048]{1,0:T(8,128)(2,1)}), bf16[2048,2048]{1,0:T(8,128)(2,1)}) %all-reduce.16.cloned.1.call-update) | async-done | bytes 8388624 | tf_op jit(solution)/shard_map/psum | solution.py:46
  964.3 12.6 fusion.59
  976.9 14.4 fusion.61
  1008.7 505.4 %while.28 = (s32[]{:T(128)}, f32[4096,1,64]{0,2,1:T(8,128)S(1)}, f32[4096,1,64]{0,2,1:T(8,128)}, f32[16,128,1,4,64]{1,0,4,3,2:T(8,128)}, bf16[16,128,1,4,64]{1,4...) while((s32[]{:T(128)}, f32[4096,1,64]{0,2,1:T(8,128)S(1)}, ...), condition=%wide.region_14.15_spmd.clone, body=%wide.region_12.14_spmd.clone.sunk | while | flops 1366298112 | bytes 104010976 | solution.py:219
  1013.0 6.2 fusion.195
  1019.2 8.0 fusion.196
  1044.4 6.2 fusion.195
  1050.6 8.0 fusion.196
  1076.0 6.2 fusion.195
  1082.2 8.0 fusion.196
  1107.6 6.2 fusion.195
  1113.8 8.0 fusion.196
  1139.2 6.2 fusion.195
  1145.4 8.0 fusion.196
  1170.9 6.2 fusion.195
  1177.1 8.0 fusion.196
  1202.4 6.2 fusion.195
  1208.6 8.0 fusion.196
  1240.2 8.0 fusion.196
  1271.8 8.0 fusion.196
  1303.4 8.0 fusion.196
  1328.8 6.2 fusion.195
  1335.0 8.0 fusion.196
  1360.3 6.2 fusion.195
  1366.5 8.0 fusion.196
  1398.1 8.0 fusion.196
  1429.7 8.0 fusion.196
  1455.0 6.2 fusion.195
  1461.2 8.0 fusion.196
  1486.6 6.2 fusion.195
  1492.8 8.0 fusion.196
  1516.6 16.8 fusion.78
  1533.5 16.8 convolution_convert_fusion.3
  1550.4 17.8 convolution_convert_fusion.4
  1575.9 9.3 fusion.94
  1593.0 9.8 fusion.88
  1603.1 17.1 convolution_convert_fusion.1
  1620.2 6.8 convolution_convert_fusion
  1631.2 25.0 %reduce-scatter.15.cloned.1.call-done = bf16[256,1280]{1,0:T(8,128)(2,1)} async-done(((bf16[2048,1280]{1,0:T(8,128)(2,1)}), bf16[256,1280]{1,0:T(8,128)(2,1)}) %reduce-scatter.15.cloned.1.call-update) | async-done | bytes 655376 | tf_op jit(solution)/shard_map/reduce_scatter | solution.py:271
  1658.4 58.0 %reduce-scatter.13.cloned.1.call-done = bf16[256,1280]{1,0:T(8,128)(2,1)} async-done(((bf16[2048,1280]{1,0:T(8,128)(2,1)}), bf16[256,1280]{1,0:T(8,128)(2,1)}) %reduce-scatter.13.cloned.1.call-update) | async-done | bytes 655376 | tf_op jit(solution)/shard_map/reduce_scatter | solution.py:268
  1718.7 37.0 %reduce-scatter.11.cloned.1.call-done = bf16[256,256]{1,0:T(8,128)(2,1)} async-done(((bf16[256,2048]{1,0:T(8,128)(2,1)}), bf16[256,256]{1,0:T(8,128)(2,1)}) %reduce-scatter.11.cloned.1.call-update) | async-done | bytes 131088 | tf_op jit(solution)/shard_map/reduce_scatter | solution.py:262
  1757.3 39.3 %psum.39 = f32[2,64]{1,0:T(2,128)} all-reduce(f32[2,64]{1,0:T(2,128)S(1)} %pad_add_fusion.1), channel_id=1, replica_groups=mesh['dp'=4,'context'=2,'tensor'=4] {'dp','context','tensor'}, use_global_device_ids=true, to_apply=%region_26.27 | all-reduce | flops 128 | bytes 1024 | tf_op jit(solution)/shard_map/psum | solution.py:256
  1799.6 564.3 %all-reduce.18.cloned.1.call-done = (bf16[2048,2048]{1,0:T(8,128)(2,1)}, bf16[2048,2048]{1,0:T(8,128)(2,1)}) async-done(((bf16[2048,2048]{1,0:T(8,128)(2,1)}, bf16[2048,2048]{1,0:T(8,128)(2,1)}), (bf16[2048,2048]{1,0:T(8,128)(2,1)}, bf16[2048,2048]{1,0:T(8,128)(2,1)})) %all-reduce.18.cloned.1.call-update) | async-done | bytes 16777232 | tf_op jit(solution)/shard_map/psum | solution.py:46
  2363.9 10.1 fusion.60
  2374.0 14.3 all-reduce.8
  2389.6 24.0 fusion.69
  (487 shorter events, 492.1 us)
Async XLA Ops:
  7.2 21.5 copy-start.22
  7.2 31.1 %all-gather.9.cloned.1.call-start = ((), (), s32[]{:S(2)}) async-start(), calls=%async_computation.6 | async-start | bytes 1769472 | tf_op jit(solution)/shard_map/all_gather | solution.py:75
  7.9 63.1 %all-gather.11.cloned.1.call-start = ((), (), s32[]{:S(2)}) async-start(), calls=%async_computation.7 | async-start | bytes 1572864 | tf_op jit(solution)/shard_map/all_gather | solution.py:103
  22.8 24.7 %copy-start.31 = (f32[8,1,256]{2,1,0:T(1,128)}, f32[8,1,256]{2,1,0:T(1,128)S(1)}, u32[]{:S(2)}) copy-start(f32[8,1,256]{2,1,0:T(1,128)S(1)} %convert_element_type.227) | copy-start | bytes 24580
  23.6 24.8 %copy-start.44 = (f32[64]{0:T(128)}, f32[64]{0:T(128)S(1)}, u32[]{:S(2)}) copy-start(f32[64]{0:T(128)S(1)} %get-tuple-element.335) | copy-start | bytes 772
  23.6 29.3 %copy-start.42 = (f32[64]{0:T(128)}, f32[64]{0:T(128)S(1)}, u32[]{:S(2)}) copy-start(f32[64]{0:T(128)S(1)} %get-tuple-element.336) | copy-start | bytes 772
  28.7 18.8 copy-start.33
  31.0 19.8 copy-start.17
  40.9 7.5 copy-start.19
  40.9 11.1 copy-start.11
  47.5 5.4 copy-start.4
  49.5 136.2 %all-gather.13.cloned.1.call-start = ((), (), s32[]{:S(2)}) async-start(), calls=%async_computation.8 | async-start | bytes 1179648 | tf_op jit(solution)/shard_map/all_gather | solution.py:76
  50.2 433.9 %all-reduce.14.cloned.1.call-start = ((), (), s32[]{:S(2)}) async-start(), calls=%async_computation.9 | async-start | bytes 16777216 | tf_op jit(solution)/shard_map/psum | solution.py:46
  183.3 9.8 copy-start.2
  183.3 9.8 copy-start.6
  183.3 9.8 copy-start.39
  183.3 9.8 copy-start.40
  185.6 7.5 copy-start.9
  193.2 332.8 %all-gather.17.cloned.1.call-start = ((), (), s32[]{:S(2)}) async-start(), calls=%async_computation.11 | async-start | bytes 5898240 | tf_op jit(solution)/shard_map/all_gather | solution.py:145
  193.8 375.1 %all-gather.15.cloned.1.call-start = ((), (), s32[]{:S(2)}) async-start(), calls=%async_computation.10 | async-start | bytes 5898240 | tf_op jit(solution)/shard_map/all_gather | solution.py:144
  194.3 418.5 %all-gather.19.cloned.1.call-start = ((), (), s32[]{:S(2)}) async-start(), calls=%async_computation.12 | async-start | bytes 5898240 | tf_op jit(solution)/shard_map/all_gather | solution.py:146
  195.1 769.2 %all-reduce.16.cloned.1.call-start = ((), (), s32[]{:S(2)}) async-start(), calls=%async_computation.13 | async-start | bytes 16777216 | tf_op jit(solution)/shard_map/psum | solution.py:46
  673.3 915.6 %reduce-scatter.7.cloned.1.call-start = ((), (), s32[]{:S(2)}) async-start(), calls=%async_computation.14 | async-start | bytes 1572864 | tf_op jit(solution)/shard_map/reduce_scatter | solution.py:235
  976.9 20.1 copy-start.20
  991.2 5.7 copy-start.1
  997.0 11.7 copy-start.3
  997.0 11.7 copy-start.7
  997.0 11.7 copy-start.12
  997.0 11.7 copy-start.23
  1013.0 6.2 copy-start
  1044.4 6.2 copy-start
  1076.0 6.2 copy-start
  1107.6 6.2 copy-start
  1139.2 6.2 copy-start
  1170.8 6.2 copy-start
  1202.4 6.2 copy-start
  1234.0 6.2 copy-start
  1265.6 6.2 copy-start
  1297.2 6.2 copy-start
  1328.8 6.2 copy-start
  1360.3 6.2 copy-start
  1391.9 6.2 copy-start
  1423.5 6.2 copy-start
  1455.0 6.2 copy-start
  1486.6 6.2 copy-start
  1516.5 112.4 %reduce-scatter.17.cloned.1.call-start = ((), (), s32[]{:S(2)}) async-start(), calls=%async_computation.19 | async-start | bytes 5898240 | tf_op jit(solution)/shard_map/reduce_scatter | solution.py:274
  1533.4 122.8 %reduce-scatter.15.cloned.1.call-start = ((), (), s32[]{:S(2)}) async-start(), calls=%async_computation.18 | async-start | bytes 5898240 | tf_op jit(solution)/shard_map/reduce_scatter | solution.py:271
  1550.3 166.1 %reduce-scatter.13.cloned.1.call-start = ((), (), s32[]{:S(2)}) async-start(), calls=%async_computation.17 | async-start | bytes 5898240 | tf_op jit(solution)/shard_map/reduce_scatter | solution.py:268
  1568.2 5.2 copy-start.5
  1568.2 5.2 copy-start.26
  1568.2 5.2 copy-start.43
  1568.2 187.5 %reduce-scatter.11.cloned.1.call-start = ((), (), s32[]{:S(2)}) async-start(), calls=%async_computation.16 | async-start | bytes 1179648 | tf_op jit(solution)/shard_map/reduce_scatter | solution.py:262
  1571.1 4.8 copy-start.10
  1585.2 7.1 copy-start.18
  1585.2 7.1 copy-start.30
  1585.2 7.1 copy-start.45
  1585.2 7.4 copy-start.38
  1585.3 7.8 copy-start.32
  1585.3 7.8 copy-start.34
  1585.3 212.6 %reduce-scatter.9.cloned.1.call-start = ((), (), s32[]{:S(2)}) async-start(), calls=%async_computation.15 | async-start | bytes 1769472 | tf_op jit(solution)/shard_map/reduce_scatter | solution.py:259
  1602.8 17.4 copy-start.24
  1602.8 761.0 %all-reduce.18.cloned.1.call-start = ((), (), s32[]{:S(2)}) async-start(), calls=%async_computation.20 | async-start | bytes 33554432 | tf_op jit(solution)/shard_map/psum | solution.py:46
  2363.9 10.1 copy-start.36
  2363.9 10.1 copy-start.41
  (14 other events, 26.6 us)
Sparse Core Ops, SparseCore 0:
  9.9 28.3 all-gather.8
  49.6 21.3 all-gather.10
  72.9 23.5 all-gather.12
  193.2 290.8 all-reduce.13
  485.8 40.1 all-gather.16
  527.7 41.1 all-gather.14
  570.7 42.0 all-gather.18
  673.4 290.8 all-reduce.15
  1516.6 19.3 reduce-scatter.6
  1539.6 56.5 reduce-scatter.16
  1599.6 56.5 reduce-scatter.14
  1659.8 56.5 reduce-scatter.12
  1719.6 36.0 reduce-scatter.10
  1758.8 39.0 reduce-scatter.8
  1800.9 562.8 all-reduce.17
where the time goes:
time: 2430 us; the launch traced here: 2420 us
  waiting for transfers between devices  1360 us (56%)
  matrix products  547 us (23%)
  other arithmetic  295 us (12%)
  local copies, waits for them, and re-layouts  124 us (5%)
  blocking collectives  80.7 us (3%)
    psum x3, waiting for transfers between devices, tensor_total(): lax.psum(partial_term.astype(jnp.bfloat16), 'tensor').astype(jnp.float32)  1130 us
    another operation x19, other arithmetic  129 us
    dot_general x32, matrix products, block_scores(): jnp.einsum('qkrd,tkd->qkrt', query_block, keys, preferred_element_type=jn...  128 us
    dot_general x16, matrix products, backward_block(): jnp.einsum('qkrt,qkrd->tkd', probs.astype(jnp.bfloat16), grad_block, pref...  87.3 us
    dynamic_update_slice x16, local copies, waits for them, and re-layouts, body(): lax.map(forward_block, (queries[member].reshape(block_count, block_rows,...  72.3 us
    reduce_scatter x1, waiting for transfers between devices, body(): lax.psum_scatter(grads[3].astype(jnp.bfloat16), ('dp', 'context'), scatte...  58 us
  transfers between devices with their start and end apart: 15, of which 12 were waited for; matrix products, arithmetic and copies ran while one was open for 12% of the time, Pallas kernels for 0%

commit v1 on v0

--- a/solution.py
+++ b/solution.py
@@ -43,7 +43,9 @@
 
 
 def tensor_total(partial_term):
-    return lax.psum(partial_term.astype(jnp.bfloat16), "tensor").astype(jnp.float32)
+    return jnp.sum(lax.all_gather(partial_term.astype(jnp.bfloat16), "tensor"), axis=0).astype(
+        jnp.float32
+    )
 
 
 def body(

time: 2430 us -> 3600 us (1.48)
  waiting for transfers between devices: 1360 us -> 2410 us
  other arithmetic: 295 us -> 350 us
    all_gather x0 -> x4, waiting for transfers between devices: none -> 2230 us  [tensor_total(): lax.all_gather(partial_term.astype(jnp.bfloat16), 'tensor')]
    psum x3 -> x0, waiting for transfers between devices: 1130 us -> none  [tensor_total(): lax.psum(partial_term.astype(jnp.bfloat16), 'tensor').astype(jnp.float32)]
    reduce_sum x0 -> x4, other arithmetic: none -> 67.4 us  [tensor_total(): jnp.sum(lax.all_gather(partial_term.astype(jnp.bfloat16), 'tensor'), axis=0)]
    reduce_scatter x1, waiting for transfers between devices: 58 us -> 0.02 us  [body(): lax.psum_scatter(grads[3].astype(jnp.bfloat16), ('dp', 'context'), scatte...]
    reduce_scatter x1, waiting for transfers between devices: 0.02 us -> 58 us  [body(): lax.psum_scatter(grads[5].astype(jnp.bfloat16), ('dp', 'context'), scatte...]
  transfers between devices with their start and end apart: 15 -> 16, of which waited for: 12 -> 13; matrix products, arithmetic and copies ran while one was open for 12% -> 9% of each run, Pallas kernels for 0% -> 0%
where the time goes in v1:
time: 3600 us; the launch traced here: 3590 us
  waiting for transfers between devices  2410 us (67%)
  matrix products  580 us (16%)
  other arithmetic  350 us (10%)
  local copies, waits for them, and re-layouts  151 us (4%)
  blocking collectives  80.1 us (2%)
    all_gather x4, waiting for transfers between devices, tensor_total(): lax.all_gather(partial_term.astype(jnp.bfloat16), 'tensor')  2230 us
    another operation x19, other arithmetic  129 us
    dot_general x32, matrix products, block_scores(): jnp.einsum('qkrd,tkd->qkrt', query_block, keys, preferred_element_type=jn...  128 us
    dot_general x16, matrix products, backward_block(): jnp.einsum('qkrt,qkrd->tkd', probs.astype(jnp.bfloat16), grad_block, pref...  87.3 us
  transfers between devices with their start and end apart: 16, of which 13 were waited for; matrix products, arithmetic and copies ran while one was open for 9% of the time, Pallas kernels for 0%

profile of v1, /device:TPU:0, one launch (start us, length us, event | category | flops | bytes accessed | tf_op | source)
XLA Modules:
  0.0 3594.0 jit_solution(18386826115833395185)
XLA Ops:
  8.6 14.2 all-gather.4
  31.0 7.3 all-gather.17.cloned.1.call-done
  40.9 6.5 fusion.89
  55.4 15.6 all-gather.19.cloned.1.call-done
  72.3 109.8 %while.27 = (s32[]{:T(128)}, bf16[16,128,1,4,64]{1,4,3,2,0:T(8,128)(2,1)}, f32[16,128,1,4]{1,3,2,0:T(4,128)}, s32[1,4096]{1,0:T(1,128)S(1)}, s32[16,128]{1,0:T(8...) while((s32[]{:T(128)}, ...), condition=%wide.region_6.7_spmd, body=%wide.region_3.6_spmd.sunk | while | flops 555748864 | bytes 27537524 | solution.py:129
  185.4 7.4 convolution_convert_fusion.2
  194.8 12.3 all-gather.5
  207.2 547.2 %all-gather.29.cloned.1.call-done = bf16[8192,2048]{1,0:T(8,128)(2,1)} async-done(((bf16[2048,2048]{1,0:T(8,128)(2,1)}), bf16[8192,2048]{1,0:T(8,128)(2,1)}) %all-gather.29.cloned.1.call-update) | async-done | bytes 33554448 | tf_op jit(solution)/shard_map/all_gather | solution.py:46
  754.4 17.4 reduce_sum.185
  771.8 8.5 multiply_reduce_fusion
  780.9 11.3 multiply_convert_fusion
  795.4 16.6 fusion.136
  812.0 26.3 all-gather.25.cloned.1.call-done
  838.3 16.5 fusion.137
  854.8 27.4 all-gather.27.cloned.1.call-done
  882.3 23.6 multiply_convert_fusion.1
  905.9 18.0 fusion.138
  923.9 17.0 add_convert_fusion
  941.4 561.1 %all-gather.33.cloned.1.call-done = bf16[8192,2048]{1,0:T(8,128)(2,1)} async-done(((bf16[2048,2048]{1,0:T(8,128)(2,1)}), bf16[8192,2048]{1,0:T(8,128)(2,1)}) %all-gather.33.cloned.1.call-update) | async-done | bytes 33554448 | tf_op jit(solution)/shard_map/all_gather | solution.py:46
  1502.4 16.5 reduce_sum.191
  1518.9 13.3 fusion.60
  1532.3 12.5 fusion.95
  1553.2 557.9 %while.28 = (s32[]{:T(128)}, f32[4096,1,64]{0,2,1:T(8,128)S(1)}, f32[4096,1,64]{0,2,1:T(8,128)}, f32[16,128,1,4,64]{1,0,4,3,2:T(8,128)}, bf16[16,128,1,4,64]{1,4...) while((s32[]{:T(128)}, f32[4096,1,64]{0,2,1:T(8,128)S(1)}, ...), condition=%wide.region_14.15_spmd.clone, body=%wide.region_12.14_spmd.clone.sunk | while | flops 1366298112 | bytes 120790224 | solution.py:221
  1563.7 8.0 fusion.201
  1592.2 6.2 fusion.200
  1598.4 8.0 fusion.201
  1633.3 8.0 fusion.201
  1661.9 6.2 fusion.200
  1668.1 8.0 fusion.201
  1703.0 8.0 fusion.201
  1731.7 6.2 fusion.200
  1737.9 8.0 fusion.201
  1766.6 6.2 fusion.200
  1772.8 8.0 fusion.201
  1801.5 6.2 fusion.200
  1807.7 8.0 fusion.201
  1842.6 8.0 fusion.201
  1877.4 8.0 fusion.201
  1906.1 6.2 fusion.200
  1912.3 8.0 fusion.201
  1947.2 8.0 fusion.201
  1982.0 8.0 fusion.201
  2016.9 8.0 fusion.201
  2051.7 8.0 fusion.201
  2080.4 6.2 fusion.200
  2086.6 8.0 fusion.201
  2113.6 17.0 convolution_convert_fusion.4
  2130.7 16.8 convolution_convert_fusion.3
  2147.5 17.6 fusion.86
  2165.2 16.8 convolution_convert_fusion.1
  2191.4 13.8 fusion.98
  2209.6 9.9 fusion.92
  2219.6 7.0 convolution_convert_fusion
  2230.8 21.6 reduce-scatter.15.cloned.1.call-done
  2254.6 58.0 %reduce-scatter.17.cloned.1.call-done = bf16[1280,256]{1,0:T(8,128)(2,1)} async-done(((bf16[1280,2048]{1,0:T(8,128)(2,1)}), bf16[1280,256]{1,0:T(8,128)(2,1)}) %reduce-scatter.17.cloned.1.call-update) | async-done | bytes 655376 | tf_op jit(solution)/shard_map/reduce_scatter | solution.py:276
  2314.8 560.8 %all-gather.31.cloned.1.call-done = bf16[8192,2048]{1,0:T(8,128)(2,1)} async-done(((bf16[2048,2048]{1,0:T(8,128)(2,1)}), bf16[8192,2048]{1,0:T(8,128)(2,1)}) %all-gather.31.cloned.1.call-update) | async-done | bytes 33554448 | tf_op jit(solution)/shard_map/all_gather | solution.py:46
  2875.6 17.0 reduce_sum.190
  2892.5 20.3 reduce-scatter.11.cloned.1.call-done
  2914.5 39.3 %psum.7 = f32[2,64]{1,0:T(2,128)} all-reduce(f32[2,64]{1,0:T(2,128)S(1)} %pad_add_fusion.1), channel_id=1, replica_groups=mesh['dp'=4,'context'=2,'tensor'=4] {'dp','context','tensor'}, use_global_device_ids=true, to_apply=%region_26.27 | all-reduce | flops 128 | bytes 1024 | tf_op jit(solution)/shard_map/psum | solution.py:258
  2956.8 561.4 %all-gather.35.cloned.1.call-done = bf16[8192,2048]{1,0:T(8,128)(2,1)} async-done(((bf16[2048,2048]{1,0:T(8,128)(2,1)}), bf16[8192,2048]{1,0:T(8,128)(2,1)}) %all-gather.35.cloned.1.call-update) | async-done | bytes 33554448 | tf_op jit(solution)/shard_map/all_gather | solution.py:46
  3518.2 16.6 reduce_sum.198
  3534.7 10.1 fusion.63
  3544.8 14.3 all-reduce.8
  3560.4 26.7 fusion.57
  (548 shorter events, 563.6 us)
Async XLA Ops:
  7.2 21.5 copy-start.22
  7.2 31.1 all-gather.17.cloned.1.call-start
  7.9 63.1 %all-gather.19.cloned.1.call-start = ((), (), s32[]{:S(2)}) async-start(), calls=%async_computation.7 | async-start | bytes 1572864 | tf_op jit(solution)/shard_map/all_gather | solution.py:105
  22.8 24.7 copy-start.36
  23.6 24.8 copy-start.53
  23.6 30.3 copy-start.51
  28.7 18.8 copy-start.38
  31.0 19.8 copy-start.18
  40.9 7.5 copy-start.20
  40.9 12.0 copy-start.10
  47.5 6.4 copy-start.5
  49.5 135.9 %all-gather.21.cloned.1.call-start = ((), (), s32[]{:S(2)}) async-start(), calls=%async_computation.8 | async-start | bytes 1179648 | tf_op jit(solution)/shard_map/all_gather | solution.py:78
  50.2 704.1 %all-gather.29.cloned.1.call-start = ((), (), s32[]{:S(2)}) async-start(), calls=%async_computation.18 | async-start | bytes 41943040 | tf_op jit(solution)/shard_map/all_gather | solution.py:46
  183.0 9.8 copy-start.2
  183.0 9.8 copy-start.7
  183.0 9.8 copy-start.48
  183.0 9.8 copy-start.49
  185.3 7.5 copy-start.12
  192.9 602.6 %all-gather.23.cloned.1.call-start = ((), (), s32[]{:S(2)}) async-start(), calls=%async_computation.9 | async-start | bytes 5898240 | tf_op jit(solution)/shard_map/all_gather | solution.py:146
  193.4 644.9 %all-gather.25.cloned.1.call-start = ((), (), s32[]{:S(2)}) async-start(), calls=%async_computation.10 | async-start | bytes 5898240 | tf_op jit(solution)/shard_map/all_gather | solution.py:147
  194.0 688.2 %all-gather.27.cloned.1.call-start = ((), (), s32[]{:S(2)}) async-start(), calls=%async_computation.11 | async-start | bytes 5898240 | tf_op jit(solution)/shard_map/all_gather | solution.py:148
  194.8 1307.7 %all-gather.33.cloned.1.call-start = ((), (), s32[]{:S(2)}) async-start(), calls=%async_computation.20 | async-start | bytes 41943040 | tf_op jit(solution)/shard_map/all_gather | solution.py:46
  207.2 1325.1 %copy-start.32 = (f32[8,1,256]{2,1,0:T(1,128)}, f32[8,1,256]{2,1,0:T(1,128)S(1)}, u32[]{:S(2)}) copy-start(f32[8,1,256]{2,1,0:T(1,128)S(1)} %convert_element_type.311) | copy-start | bytes 24580
  780.9 751.3 %copy-start.34 = (f32[2048]{0:T(1024)}, f32[2048]{0:T(1024)S(1)}, u32[]{:S(2)}) copy-start(f32[2048]{0:T(1024)S(1)} %fusion.131) | copy-start | bytes 24580
  905.9 18.0 copy-start.55
  940.9 1264.4 %reduce-scatter.7.cloned.1.call-start = ((), (), s32[]{:S(2)}) async-start(), calls=%async_computation.12 | async-start | bytes 1572864 | tf_op jit(solution)/shard_map/reduce_scatter | solution.py:237
  1518.9 13.3 copy-start.45
  1518.9 13.3 copy-start.4
  1518.9 13.3 copy-start.25
  1532.3 12.6 copy-start.46
  1532.3 20.9 copy-start.3
  1532.3 20.9 copy-start.8
  1532.3 20.9 copy-start.11
  1532.3 20.9 copy-start.23
  1556.8 6.9 copy-start
  1591.5 6.8 copy-start
  1626.4 6.9 copy-start
  1661.3 6.8 copy-start
  1696.1 6.8 copy-start
  1731.0 6.9 copy-start
  1765.9 6.9 copy-start
  1800.8 6.9 copy-start
  1835.7 6.9 copy-start
  1870.6 6.9 copy-start
  1905.4 6.9 copy-start
  1940.3 6.9 copy-start
  1975.1 6.8 copy-start
  2010.0 6.9 copy-start
  2044.9 6.8 copy-start
  2079.7 6.9 copy-start
  2113.6 115.0 %reduce-scatter.13.cloned.1.call-start = ((), (), s32[]{:S(2)}) async-start(), calls=%async_computation.15 | async-start | bytes 5898240 | tf_op jit(solution)/shard_map/reduce_scatter | solution.py:270
  2130.6 121.8 %reduce-scatter.15.cloned.1.call-start = ((), (), s32[]{:S(2)}) async-start(), calls=%async_computation.16 | async-start | bytes 5898240 | tf_op jit(solution)/shard_map/reduce_scatter | solution.py:273
  2147.5 165.1 %reduce-scatter.17.cloned.1.call-start = ((), (), s32[]{:S(2)}) async-start(), calls=%async_computation.17 | async-start | bytes 5898240 | tf_op jit(solution)/shard_map/reduce_scatter | solution.py:276
  2165.1 710.5 %all-gather.31.cloned.1.call-start = ((), (), s32[]{:S(2)}) async-start(), calls=%async_computation.19 | async-start | bytes 41943040 | tf_op jit(solution)/shard_map/all_gather | solution.py:46
  2182.0 730.9 %reduce-scatter.11.cloned.1.call-start = ((), (), s32[]{:S(2)}) async-start(), calls=%async_computation.14 | async-start | bytes 1179648 | tf_op jit(solution)/shard_map/reduce_scatter | solution.py:264
  2191.4 16.4 copy-start.19
  2191.4 16.4 copy-start.31
  2191.4 16.4 copy-start.54
  2191.4 16.7 copy-start.43
  2205.2 749.9 %reduce-scatter.9.cloned.1.call-start = ((), (), s32[]{:S(2)}) async-start(), calls=%async_computation.13 | async-start | bytes 1769472 | tf_op jit(solution)/shard_map/reduce_scatter | solution.py:261
  2209.5 10.0 copy-start.24
  2219.5 1298.6 %all-gather.35.cloned.1.call-start = ((), (), s32[]{:S(2)}) async-start(), calls=%async_computation.21 | async-start | bytes 41943040 | tf_op jit(solution)/shard_map/all_gather | solution.py:46
  3534.7 10.1 copy-start.50
  3534.7 25.7 copy-start.41
  (42 other events, 102.6 us)
Sparse Core Ops, SparseCore 0:
  9.9 28.3 all-gather.16
  49.6 21.3 all-gather.18
  72.9 23.5 all-gather.20
  192.9 561.3 all-gather.28
  756.1 39.2 all-gather.22
  797.2 41.1 all-gather.24
  840.2 42.0 all-gather.26
  941.0 561.3 all-gather.32
  2113.7 18.4 reduce-scatter.6
  2135.8 56.5 reduce-scatter.12
  2195.8 56.5 reduce-scatter.14
  2256.0 56.5 reduce-scatter.16
  2314.2 561.3 all-gather.30
  2878.6 34.2 reduce-scatter.10
  2916.0 39.0 reduce-scatter.8
  2957.1 561.0 all-gather.34
